TPU v7x, 256 devices: a whole 4x4x8 slice. The times are simulated.
256 devices in a mesh: seq: 64 (over x, z, core), head: 4 (over y).
Axes of the slice: x: 4, y: 4, z: 8, core: 2. Of those that a mesh axis runs over, the one named last changes fastest.
Arguments:
- tokens: bfloat16 [21504, 4096], P('seq', 'head')
- w_short: float32 [3, 4096], P(None, 'head'), may hold values from 0.25 to 1.5
- w_query: bfloat16 [4096, 2048], P(None, 'head')
- w_key: bfloat16 [4096, 2048], P(None, 'head')
- w_value: bfloat16 [4096, 2048], P(None, 'head'), may hold values from -0.09375 to 0.09375
- owner_lengths: int32 [64], replicated, may hold values from 1 to 224, as said below
Outputs:
- attended: bfloat16 [14336, 2048], P('seq', 'head')
Inputs may be any that keep to these rules, and one draw needn't show every extreme that they name: The counts sum to 7168; owner o holds the coarse rows from starts[o] on, with o * 112 <= starts[o] and starts[o] + owner_lengths[o] <= (o + 2) * 112; the largest count is exactly 224.
All inputs are finite; a program needn't handle non-finite values.
Results may differ from a plain program's by a relative error of at most 0.012.
The roundings to bfloat16 on the way count: a program that leaves them out, or rounds other values in their place, can miss the bound.
Values may be sent and summed in bfloat16 or wider, within the bound.
A program may use at most 128 MiB of HBM per device.

v0:
```python
import math

import jax
import jax.numpy as jnp
from jax import lax
from jax.sharding import PartitionSpec as P

HD = 128


masked_score = -1e30


def from_behind(x, axis, by):
    devices = lax.axis_size(axis)
    pairs = [(i, i + by) for i in range(devices) if 0 <= i + by < devices]
    return lax.ppermute(x, axis, pairs)


def block_scores(owned, key_block, offset, query_pos):
    length = key_block.shape[0]
    keyed = key_block.reshape(length, owned.shape[1], HD)
    scores = jnp.einsum("qhd,khd->hqk", owned, keyed, preferred_element_type=jnp.float32) * (
        1.0 / math.sqrt(HD)
    )
    key_pos = offset + jnp.arange(length, dtype=jnp.int32)
    allowed = key_pos[None, :] <= query_pos[:, None]
    return jnp.where(allowed[None], scores, masked_score)


def block_context(owned, key_block, value_block, offset, query_pos, maxima):
    scores = block_scores(owned, key_block, offset, query_pos)
    weights = jnp.exp(scores - maxima[:, :, None])
    length = value_block.shape[0]
    valued = value_block.reshape(length, owned.shape[1], HD)
    added = jnp.einsum(
        "hqk,khd->hqd", weights.astype(jnp.bfloat16), valued, preferred_element_type=jnp.float32
    )
    return (jnp.sum(weights, axis=2), added)


def shards(tokens, w_short, w_query, w_key, w_value, owner_lengths):
    rows_local = tokens.shape[0]
    coarse_local = rows_local // 3
    width_part = tokens.shape[1]
    seq_count = lax.axis_size("seq")
    position = lax.axis_index("seq")
    boundary = from_behind(tokens[rows_local - 2 :], "seq", 1)
    shifted = jnp.concatenate([boundary, tokens[: rows_local - 2]], axis=0)
    grouped = shifted.reshape(coarse_local, 3, width_part)
    pooled = (
        grouped[:, 0].astype(jnp.float32) * w_short[0]
        + grouped[:, 1].astype(jnp.float32) * w_short[1]
        + grouped[:, 2].astype(jnp.float32) * w_short[2]
    )
    squares = lax.psum(jnp.sum(pooled * pooled, axis=1), "head")
    full_width = width_part * lax.axis_size("head")
    norm_scale = lax.rsqrt(squares / full_width + 1e-05)
    coarse_part = (pooled * norm_scale[:, None]).astype(jnp.bfloat16)
    features = w_query.shape[1]
    zero_sums = jnp.zeros((coarse_local, features), jnp.float32)
    carried = (zero_sums, zero_sums, zero_sums)
    shard_rows = lax.all_gather(coarse_part, "head", axis=1, tiled=True)
    outputs = []
    for running, weight in zip(carried, (w_query, w_key, w_value)):
        outputs.append(jnp.dot(shard_rows, weight, preferred_element_type=jnp.float32))
    query_sum, key_sum, value_sum = tuple(outputs)
    queries = query_sum.astype(jnp.bfloat16)
    key_rows = key_sum.astype(jnp.bfloat16)
    value_rows = value_sum.astype(jnp.bfloat16)
    starts = jnp.cumsum(owner_lengths) - owner_lengths
    owners = jnp.arange(seq_count, dtype=jnp.int32)
    chosen = owners == position
    first_row = jnp.sum(jnp.where(chosen, starts, 0))
    row_count = jnp.sum(jnp.where(chosen, owner_lengths, 0))
    capacity = 2 * coarse_local
    following = from_behind(queries, "seq", -1)
    window = jnp.concatenate(
        [queries, following, jnp.zeros((coarse_local, features), jnp.bfloat16)], axis=0
    )
    local_start = first_row - position * coarse_local
    owned_rows = lax.dynamic_slice_in_dim(window, local_start, capacity, 0)
    head_count = features // HD
    owned = owned_rows.reshape(capacity, head_count, HD)
    query_pos = first_row + jnp.arange(capacity, dtype=jnp.int32)
    last_row = first_row + row_count
    coarse_total = seq_count * coarse_local
    start_max = jnp.full((head_count, capacity), masked_score, jnp.float32)
    start_sums = (
        jnp.zeros((head_count, capacity), jnp.float32),
        jnp.zeros((head_count, capacity, HD), jnp.float32),
    )
    key_all, value_all = (
        lax.all_gather(key_rows, "seq", axis=0, tiled=True),
        lax.all_gather(value_rows, "seq", axis=0, tiled=True),
    )
    block_size = math.gcd(coarse_total, 512)
    blocks = (last_row + block_size - 1) // block_size

    def find_max(index, maxima):
        key_block = lax.dynamic_slice_in_dim(key_all, index * block_size, block_size, 0)
        return jnp.maximum(
            maxima, jnp.max(block_scores(owned, key_block, index * block_size, query_pos), axis=2)
        )

    maxima = lax.fori_loop(0, blocks, find_max, start_max)

    def add_block(index, carried):
        offset = index * block_size
        key_block = lax.dynamic_slice_in_dim(key_all, offset, block_size, 0)
        value_block = lax.dynamic_slice_in_dim(value_all, offset, block_size, 0)
        sums, added = block_context(owned, key_block, value_block, offset, query_pos, maxima)
        return (carried[0] + sums, carried[1] + added)

    totals, context = lax.fori_loop(0, blocks, add_block, start_sums)
    result = (context / totals[:, :, None]).transpose(1, 0, 2).reshape(capacity, features)
    live = jnp.arange(capacity, dtype=jnp.int32) < row_count
    return jnp.where(live[:, None], result, 0.0).astype(jnp.bfloat16)


def solution(mesh):
    return jax.shard_map(
        shards,
        mesh=mesh,
        in_specs=(
            P("seq", "head"),
            P(None, "head"),
            P(None, "head"),
            P(None, "head"),
            P(None, "head"),
            P(),
        ),
        out_specs=P("seq", "head"),
        check_vma=False,
    )
```

profile of v0, /device:TPU:199, one launch (start us, length us, event | category | flops | bytes accessed | tf_op | source)
XLA Modules:
  0.0 273.7 jit_solution(7263793353940745998)
XLA Ops:
  7.3 3.2 %collective-permute-start = (bf16[2,1024]{1,0:T(2,128)(2,1)S(1)}, bf16[2,1024]{1,0:T(2,128)(2,1)S(1)}, u32[]{:S(2)}, u32[]{:S(2)}) collective-permute-start(bf16[2,1024]{1,0:T(2,128)(2,1)S(1)} %slice.24), channel_id=1, source_target_pairs={{0,4},{4,8},{8,12},{12,16},{16,20},{20,24},{24,28},{28,32},{32,36}... | collective-permute-start | bytes 12296 | tf_op jit(solution)/shard_map/ppermute | solution.py:17
  11.3 1.3 pad_maximum_fusion
  14.4 8.7 %psum.7 = f32[112]{0:T(128)S(1)} all-reduce(f32[112]{0:T(128)S(1)} %get-tuple-element.175), channel_id=1, replica_groups=mesh['seq'=64,'head'=4] {'head'}, use_global_device_ids=true, to_apply=%region_4.5 | all-reduce | flops 112 | bytes 896 | tf_op jit(solution)/shard_map/psum | solution.py:56
  23.3 12.6 %all_gather.9 = bf16[112,4096]{1,0:T(8,128)(2,1)S(1)} all-gather(bf16[112,1024]{1,0:T(8,128)(2,1)S(1)} %multiply_convert_fusion), channel_id=1, replica_groups=mesh['seq'=64,'head'=4] {'head'}, dimensions={1}, use_global_device_ids=true | all-gather | bytes 1146880 | tf_op jit(solution)/shard_map/all_gather | solution.py:63
  35.9 3.6 %convolution_convert_fusion.2 = bf16[112,512]{1,0:T(8,128)(2,1)} fusion(bf16[112,4096]{1,0:T(8,128)(2,1)S(1)} %all_gather.9, bf16[4096,512]{1,0:T(8,128)(2,1)} %param.13), kind=kOutput, calls=%fused_computation.20 | convolution fusion | flops 469819392 | bytes 5226496 | tf_op jit(solution)/shard_map/dot_general | solution.py:66
  39.6 3.6 %convolution_convert_fusion = bf16[112,512]{1,0:T(8,128)(2,1)} fusion(bf16[112,4096]{1,0:T(8,128)(2,1)S(1)} %all_gather.9, bf16[4096,512]{1,0:T(8,128)(2,1)} %param.14), kind=kOutput, calls=%fused_computation.18 | convolution fusion | flops 469819392 | bytes 5226496 | tf_op jit(solution)/shard_map/dot_general | solution.py:66
  44.2 2.9 %convolution_convert_fusion.1 = bf16[112,512]{1,0:T(8,128)(2,1)S(1)} fusion(bf16[112,4096]{1,0:T(8,128)(2,1)S(1)} %all_gather.9, bf16[4096,512]{1,0:T(8,128)(2,1)} %param.12), kind=kOutput, calls=%fused_computation.19 | convolution fusion | flops 469819392 | bytes 5226496 | tf_op jit(solution)/shard_map/dot_general | solution.py:66
  47.2 6.4 %collective-permute-start.1 = (bf16[112,512]{1,0:T(8,128)(2,1)S(1)}, bf16[112,512]{1,0:T(8,128)(2,1)S(1)}, u32[]{:S(2)}, u32[]{:S(2)}) collective-permute-start(bf16[112,512]{1,0:T(8,128)(2,1)S(1)} %convolution_convert_fusion.1), channel_id=1, source_target_pairs={{4,0},{8,4},{12,8},{16,12},{20,16},{24,20},{28,24},{32,28},{36,32}... | collective-permute-start | bytes 344072 | tf_op jit(solution)/shard_map/ppermute | solution.py:17
  56.3 1.3 collective-permute-done.1
  57.8 65.8 %all-gather.3.cloned.1.call-done = bf16[7168,512]{1,0:T(8,128)(2,1)} async-done(((bf16[112,512]{1,0:T(8,128)(2,1)}), bf16[7168,512]{1,0:T(8,128)(2,1)}) %all-gather.3.cloned.1.call-update) | async-done | bytes 7340048 | tf_op jit(solution)/shard_map/all_gather | solution.py:94
  123.5 10.1 %copy.19 = bf16[7168,512]{0,1:T(8,128)(2,1)} copy(bf16[7168,512]{1,0:T(8,128)(2,1)} %all-gather.3.cloned.1.call-done) | data formatting | bytes 14680064
  133.6 33.0 %while.24 = (s32[]{:T(128)}, f32[4,224]{1,0:T(4,128)S(1)}, s32[]{:T(128)}, bf16[7168,512]{0,1:T(8,128)(2,1)}, bf16[224,4,128]{2,0,1:T(8,128)(2,1)S(1)}, /*index=...) while((s32[]{:T(128)}, f32[4,224]{1,0:T(4,128)S(1)}, s32[]{:T(128)}, ...), condition=%wide.region_7.8_spmd.clone, body=%wide.region_5.7_spmd.clone.sunk | while | flops 118932200 | bytes 2052007 | solution.py:106
  135.9 1.1 constant_dynamic-slice_fusion.6
  138.3 1.1 constant_dynamic-slice_fusion.6
  140.7 1.1 constant_dynamic-slice_fusion.6
  143.0 1.1 constant_dynamic-slice_fusion.6
  145.4 1.1 constant_dynamic-slice_fusion.6
  147.7 1.1 constant_dynamic-slice_fusion.6
  150.1 1.1 constant_dynamic-slice_fusion.6
  152.5 1.1 constant_dynamic-slice_fusion.6
  154.8 1.1 constant_dynamic-slice_fusion.6
  157.2 1.1 constant_dynamic-slice_fusion.6
  159.5 1.1 constant_dynamic-slice_fusion.6
  161.9 1.1 constant_dynamic-slice_fusion.6
  164.3 1.1 constant_dynamic-slice_fusion.6
  166.6 38.5 %all-gather.5.cloned.1.call-done = bf16[7168,512]{1,0:T(8,128)(2,1)} async-done(((bf16[112,512]{1,0:T(8,128)(2,1)}), bf16[7168,512]{1,0:T(8,128)(2,1)}) %all-gather.5.cloned.1.call-update) | async-done | bytes 7340048 | tf_op jit(solution)/shard_map/all_gather | solution.py:95
  205.2 60.7 %while.25 = (s32[]{:T(128)}, f32[4,224]{1,0:T(4,128)S(1)}, f32[4,224,128]{2,1,0:T(8,128)S(1)}, s32[]{:T(128)}, bf16[7168,512]{0,1:T(8,128)(2,1)}, /*index=5*/bf1...) while((s32[]{:T(128)}, f32[4,224]{1,0:T(4,128)S(1)}, ...), condition=%wide.region_10.11_spmd.clone, body=%wide.region_8.10_spmd.clone.sunk | while | flops 237404896 | bytes 7429571 | solution.py:115
  205.2 1.1 constant_dynamic-slice_fusion.7
  207.8 1.1 constant_dynamic-slice_fusion.8
  209.5 1.1 constant_dynamic-slice_fusion.7
  212.1 1.1 constant_dynamic-slice_fusion.8
  213.9 1.1 constant_dynamic-slice_fusion.7
  216.5 1.1 constant_dynamic-slice_fusion.8
  218.2 1.1 constant_dynamic-slice_fusion.7
  220.8 1.1 constant_dynamic-slice_fusion.8
  222.5 1.1 constant_dynamic-slice_fusion.7
  225.1 1.1 constant_dynamic-slice_fusion.8
  226.9 1.1 constant_dynamic-slice_fusion.7
  229.5 1.1 constant_dynamic-slice_fusion.8
  231.2 1.1 constant_dynamic-slice_fusion.7
  233.8 1.1 constant_dynamic-slice_fusion.8
  238.1 1.1 constant_dynamic-slice_fusion.8
  242.5 1.1 constant_dynamic-slice_fusion.8
  246.8 1.1 constant_dynamic-slice_fusion.8
  251.1 1.1 constant_dynamic-slice_fusion.8
  255.5 1.1 constant_dynamic-slice_fusion.8
  259.8 1.1 constant_dynamic-slice_fusion.8
  264.2 1.1 constant_dynamic-slice_fusion.8
  (202 shorter events, 62.0 us)
Async XLA Ops:
  6.5 117.0 %all-gather.3.cloned.1.call-start = ((), (), s32[]{:S(2)}) async-start(), calls=%async_computation | async-start | bytes 7454720 | tf_op jit(solution)/shard_map/all_gather | solution.py:94
  7.3 4.1 %collective-permute-start = (bf16[2,1024]{1,0:T(2,128)(2,1)S(1)}, bf16[2,1024]{1,0:T(2,128)(2,1)S(1)}, u32[]{:S(2)}, u32[]{:S(2)}) collective-permute-start(bf16[2,1024]{1,0:T(2,128)(2,1)S(1)} %slice.24), channel_id=1, source_target_pairs={{0,4},{4,8},{8,12},{12,16},{16,20},{20,24},{24,28},{28,32},{32,36}... | collective-permute-start | bytes 12296 | tf_op jit(solution)/shard_map/ppermute | solution.py:17
  35.9 7.3 %copy-start = (s32[64]{0:T(128)S(1)}, s32[64]{0:T(128)}, u32[]{:S(2)}) copy-start(s32[64]{0:T(128)} %param.15) | copy-start | bytes 772
  39.5 165.6 %all-gather.5.cloned.1.call-start = ((), (), s32[]{:S(2)}) async-start(), calls=%async_computation.1 | async-start | bytes 7454720 | tf_op jit(solution)/shard_map/all_gather | solution.py:95
  47.2 10.4 %collective-permute-start.1 = (bf16[112,512]{1,0:T(8,128)(2,1)S(1)}, bf16[112,512]{1,0:T(8,128)(2,1)S(1)}, u32[]{:S(2)}, u32[]{:S(2)}) collective-permute-start(bf16[112,512]{1,0:T(8,128)(2,1)S(1)} %convolution_convert_fusion.1), channel_id=1, source_target_pairs={{4,0},{8,4},{12,8},{16,12},{20,16},{24,20},{28,24},{32,28},{36,32}... | collective-permute-start | bytes 344072 | tf_op jit(solution)/shard_map/ppermute | solution.py:17
Sparse Core Ops, SparseCore 0:
  39.6 83.8 all-gather.2
  126.3 78.8 all-gather.4
where the time goes:
time: 277 us; the launch traced here: 274 us
  waiting for transfers between devices  106 us (38%)
  local copies, waits for them, and re-layouts  60.7 us (22%)
  matrix products  33.8 us (12%)
  other arithmetic  25.7 us (9%)
  blocking collectives  21.3 us (8%)
  between operations  15.4 us (6%)
  starting transfers between devices  9.67 us (3%)
    all_gather x1, waiting for transfers between devices, shards(): lax.all_gather(key_rows, 'seq', axis=0, tiled=True)  65.8 us
    all_gather x1, waiting for transfers between devices, shards(): lax.all_gather(value_rows, 'seq', axis=0, tiled=True)  38.5 us
    dynamic_slice x28, local copies, waits for them, and re-layouts, add_block(): value_block = lax.dynamic_slice_in_dim(value_all, offset, block_size, 0)  18.1 us
    dot_general x28, matrix products, block_scores(): jnp.einsum('qhd,khd->hqk', owned, keyed, preferred_element_type=jnp.float32)  17.6 us
    add x28, other arithmetic, shards(): query_pos = first_row + jnp.arange(capacity, dtype=jnp.int32)  16.1 us
    dynamic_slice x14, local copies, waits for them, and re-layouts, find_max(): lax.dynamic_slice_in_dim(key_all, index * block_size, block_size, 0)  15.2 us
    dynamic_slice x14, local copies, waits for them, and re-layouts, add_block(): key_block = lax.dynamic_slice_in_dim(key_all, offset, block_size, 0)  15.1 us
    all_gather x1, blocking collectives, shards(): shard_rows = lax.all_gather(coarse_part, 'head', axis=1, tiled=True)  12.6 us
  transfers between devices with their start and end apart: 4, of which 3 were waited for; matrix products, arithmetic and copies ran while one was open for 19% of the time, Pallas kernels for 0%

commit v1 on v0

v1 whole, which is shorter than its diff:
```python
import functools
import math

import jax
import jax.numpy as jnp
from jax import lax
from jax.experimental import pallas as pl
from jax.experimental.pallas import tpu as pltpu
from jax.sharding import PartitionSpec as P

HD = 128
NX = 4
NY = 4
MASKED = -1e30
F32 = jnp.float32
BF16 = jnp.bfloat16
DORDER = (0, 1, 3, 2)


def layer_kernel(
    seqs, width,
    tokens, w_short, w_q, w_k, w_v, lengths,
    out,
    tok, tok32, pooled, part, sums, coarse, weights, acc, kv_out, q_out, kv, q_all,
    m_s, l_s, o_s, ctx, win,
    tok_sem, w_sem, bnd_sem, ss_send, ss_recv, y_send, y_recv,
    s2_send, s2_recv, q_send, q_recv, cw_send, cw_recv, ccw_send, ccw_recv,
    pt_send, pt_recv, o_send, o_recv, n_send, n_recv,
):
    NZ = seqs // (2 * NX)
    NT = NZ // 2
    NZC = 2 * NZ
    rows, part_width = tok.shape
    CD = rows // 3
    lane_blocks = part_width // 128
    half = part_width // 2
    features = NX * HD

    s = lax.axis_index("seq")
    y = lax.axis_index("head")
    x = s // NZC
    zc = s % NZC
    z = zc // 2
    c = zc % 2

    def seq_id(xx, zz, cc):
        return (xx * NZ + zz) * 2 + cc

    def at_seq(i):
        return (i, y)

    def remote(src, dst, send, recv, device):
        return pltpu.make_async_remote_copy(
            src_ref=src, dst_ref=dst, send_sem=send, recv_sem=recv,
            device_id=device, device_id_type=pl.DeviceIdType.MESH,
        )

    z_up = seq_id(x, (z + 1) % NZ, c)
    z_down = seq_id(x, (z + NZ - 1) % NZ, c)
    partner = seq_id(x, z, 1 - c)

    def x_peer(d):
        return ((x + d) % NX) * NZC + zc

    barrier = pltpu.get_barrier_semaphore()
    greeted = [((s + seqs - 1) % seqs, y)]
    greeted += [(s, (y + d) % NY) for d in (1, 2, 3)]
    greeted += [(x_peer(d), y) for d in (1, 2, 3)]
    greeted += [(z_up, y), (z_down, y), (partner, y)]
    greeted += [(((x + d) % NX) * NZC + (zc + 1) % NZC, y) for d in range(NX)]
    for device in greeted:
        pl.semaphore_signal(barrier, inc=1, device_id=device, device_id_type=pl.DeviceIdType.MESH)

    tail = 16
    tail_copy = pltpu.make_async_copy(
        tokens.at[pl.ds(rows - tail, tail)], tok.at[pl.ds(rows - tail, tail)], tok_sem.at[0])
    head_copy = pltpu.make_async_copy(
        tokens.at[pl.ds(0, rows - tail)], tok.at[pl.ds(0, rows - tail)], tok_sem.at[1])
    tail_copy.start()
    head_copy.start()
    y_of_slot = [y, (y + 3) % NY, (y + 1) % NY, (y + 2) % NY]
    w_copies = []
    for slot in range(4):
        for j, w in enumerate((w_k, w_v, w_q)):
            rows_w = pl.ds(pl.multiple_of(y_of_slot[slot] * part_width, part_width), part_width)
            cp = pltpu.make_async_copy(w.at[rows_w], weights.at[slot, j], w_sem.at[slot, j])
            cp.start()
            w_copies.append(cp)

    tail_copy.wait()
    for b in range(lane_blocks):
        tok32[b, pl.ds(rows - 8, 16), :] = tok[pl.ds(rows - tail, tail), pl.ds(b * 128, 128)].astype(F32)
    pl.semaphore_wait(barrier, len(greeted))
    bnd = remote(
        tok32.at[:, pl.ds(rows, 8), :], tok32.at[:, pl.ds(0, 8), :],
        bnd_sem.at[0], bnd_sem.at[1], at_seq((s + 1) % seqs))
    bnd.start()
    head_copy.wait()
    for b in range(lane_blocks):
        tok32[b, pl.ds(8, rows - tail), :] = tok[pl.ds(0, rows - tail), pl.ds(b * 128, 128)].astype(F32)
    bnd.wait_recv()

    @pl.when(s == 0)
    def _():
        tok32[:, pl.ds(0, 8), :] = jnp.zeros((lane_blocks, 8, 128), F32)

    part[...] = jnp.zeros_like(part)
    square = jnp.zeros((CD, 128), F32)
    for b in range(lane_blocks):
        lanes = pl.ds(b * 128, 128)
        first = tok32[b, pl.ds(6, CD, stride=3), :]
        second = tok32[b, pl.ds(7, CD, stride=3), :]
        third = tok32[b, pl.ds(8, CD, stride=3), :]
        p = first * w_short[0:1, lanes] + second * w_short[1:2, lanes] + third * w_short[2:3, lanes]
        pooled[b] = p
        square = square + p * p
    part[pl.ds(0, CD), :] = square
    sums[0] = jnp.broadcast_to(jnp.sum(part[...].T, axis=0, keepdims=True), (8, 128))
    ss = []
    for d in (1, 2, 3):
        cp = remote(sums.at[0], sums.at[d], ss_send.at[d - 1], ss_recv.at[d - 1], (s, (y + d) % NY))
        cp.start()
        ss.append(cp)
    for cp in ss:
        cp.wait_recv()
    total = sums[0] + sums[1] + sums[2] + sums[3]
    scale_row = lax.rsqrt(total / width + 1e-05)
    part[...] = jnp.broadcast_to(scale_row[0:1], (128, 128))
    scale = part[...].T[0:CD]
    for b in range(lane_blocks):
        h, o = divmod(b * 128, half)
        coarse[0, h, :, pl.ds(o, 128)] = (pooled[b] * scale).astype(BF16)

    y_up = (s, (y + 1) % NY)
    y_down = (s, (y + 3) % NY)
    sends = []

    def y_copy(src, dst, h, i, device):
        r = (dst - 1) * 2 + h
        return remote(coarse.at[src, h], coarse.at[dst, h], y_send.at[i], y_recv.at[r], device)

    own = [y_copy(0, 1, 0, 0, y_up), y_copy(0, 2, 1, 1, y_down), y_copy(0, 1, 1, 2, y_up), y_copy(0, 2, 0, 3, y_down)]
    for cp in own:
        cp.start()
        sends.append(cp)
    relay = [y_copy(1, 3, 0, 4, y_up), y_copy(2, 3, 1, 5, y_down)]

    def wait_block(slot, h):
        y_copy(slot, slot, h, 0, y_up).wait_recv()

    def project(slot, h, j):
        w = weights[slot, j, pl.ds(h * half, half), :]
        return jnp.dot(coarse[slot, h], w, preferred_element_type=F32)

    def add_block(slot, h):
        for j in range(3):
            acc[j] = acc[j] + project(slot, h, j)

    for j in range(3):
        w_copies[j].wait()
        acc[j] = jnp.dot(coarse[0, 0], weights[0, j, pl.ds(0, half), :], preferred_element_type=F32)
    wait_block(1, 0)
    relay[0].start()
    wait_block(2, 1)
    relay[1].start()
    sends += relay
    add_block(0, 1)
    for cp in w_copies[3:]:
        cp.wait()
    add_block(1, 0)
    add_block(2, 1)
    wait_block(1, 1)
    add_block(1, 1)
    wait_block(2, 0)
    add_block(2, 0)
    wait_block(3, 0)
    add_block(3, 0)
    wait_block(3, 1)

    def x_abs(d):
        return (x + d) % NX

    def block_rows(xx):
        return pl.ds(pl.multiple_of(xx * CD, CD), CD)

    def sub(slot, d):
        return kv.at[slot, :, block_rows(x_abs(d)), :]

    for j in range(2):
        r = (acc[j] + project(3, 1, j)).astype(BF16)
        for h in range(NX):
            kv_out[h, j] = r[:, h * HD:(h + 1) * HD]
    for d in (1, 3, 2):
        cp = remote(
            kv_out.at[x_abs(d)], kv.at[0, :, block_rows(x), :],
            s2_send.at[d - 1], s2_recv.at[NX - d - 1], at_seq(x_peer(d)))
        cp.start()
        sends.append(cp)
    own_kv = kv_out[x]
    kv[0, :, block_rows(x), :] = own_kv

    def ring_copy(up, src_slot, t_next, dst_slot, i, d):
        send = cw_send if up else ccw_send
        recv = cw_recv if up else ccw_recv
        return remote(
            sub(src_slot, d), sub(dst_slot, d), send.at[t_next - 1, i], recv.at[t_next - 1, i],
            at_seq(z_up if up else z_down))

    def partner_copy(slot, i, d):
        return remote(sub(slot, d), sub(NZ + slot, d), pt_send.at[slot, i], pt_recv.at[slot, i], at_seq(partner))

    last = NZ - 1

    def start_ring(i, d):
        for up in (True, False):
            if NT > 1:
                ring_copy(up, 0, 1, 1 if up else NT, i, d).start()
            elif (i < 2) == up:
                ring_copy(up, 0, 1, last, i, d).start()
        partner_copy(0, i, d).start()

    start_ring(0, 0)

    r = (acc[2] + project(3, 1, 2)).astype(BF16)
    for h in range(NX):
        q_out[h] = r[:, h * HD:(h + 1) * HD]
    for d in (1, 3, 2):
        cp = remote(
            q_out.at[x_abs(d)], q_all.at[x], q_send.at[d - 1], q_recv.at[NX - d - 1], at_seq(x_peer(d)))
        cp.start()
        sends.append(cp)
    q_all[x] = q_out[x]

    for i, d in enumerate(DORDER):
        if d:
            remote(sub(0, d), sub(0, d), s2_send.at[0], s2_recv.at[d - 1], at_seq(partner)).wait_recv()
            start_ring(i, d)
    for d in (1, 3, 2):
        remote(q_all.at[x_abs(d)], q_all.at[x_abs(d)], q_send.at[0], q_recv.at[d - 1], at_seq(partner)).wait_recv()

    inverse = 1.0 / math.sqrt(HD)

    def attend(slot, allowed, first=False):
        for xq in range(NX):
            nk = (xq + 1) * CD
            keys = kv[slot, 0, pl.ds(0, nk), :]
            values = kv[slot, 1, pl.ds(0, nk), :]
            sc = lax.dot_general(q_all[xq], keys, (((1,), (1,)), ((), ())), preferred_element_type=F32) * inverse
            column = lax.broadcasted_iota(jnp.int32, (CD, nk), 1)
            if first:
                limit = lax.broadcasted_iota(jnp.int32, (CD, nk), 0) + (xq * CD + 1)
            else:
                limit = jnp.where(allowed, nk, xq * CD)
            sc = jnp.where(column < limit, sc, MASKED)
            top = jnp.max(sc, axis=1, keepdims=True)
            if not first:
                old = m_s[xq]
                new = jnp.maximum(old, top)
                alpha = jnp.exp(old - new)
                m_s[xq] = new
                top = new[:, 0:1]
            else:
                m_s[xq] = jnp.broadcast_to(top, (CD, HD))
            w = jnp.exp(sc - top)
            added = jnp.dot(w.astype(BF16), values, preferred_element_type=F32)
            lw = jnp.sum(w, axis=1, keepdims=True)
            if first:
                l_s[xq] = jnp.broadcast_to(lw, (CD, HD))
                o_s[xq] = added
            else:
                l_s[xq] = l_s[xq] * alpha + lw
                o_s[xq] = o_s[xq] * alpha + added

    def wait_partner(slot):
        for i, d in enumerate(DORDER):
            remote(sub(NZ + slot, d), sub(NZ + slot, d), pt_send.at[slot, i], pt_recv.at[slot, i], at_seq(partner)).wait_recv()

    attend(0, None, first=True)
    wait_partner(0)
    attend(NZ, c == 1)

    def arrived(up, t, slot, i, d):
        recv = cw_recv if up else ccw_recv
        send = cw_send if up else ccw_send
        remote(sub(slot, d), sub(slot, d), send.at[t - 1, i], recv.at[t - 1, i], at_seq(partner)).wait_recv()

    def ring_step(t, carry):
        for i, d in enumerate(DORDER):
            for up in (True, False):
                slot = t if up else NT - 1 + t
                arrived(up, t, slot, i, d)

                @pl.when(t + 1 < NT)
                def _():
                    ring_copy(up, slot, t + 1, slot + 1, i, d).start()

                if (i < 2) == up:
                    @pl.when(t + 1 == NT)
                    def _():
                        ring_copy(up, slot, t + 1, last, i, d).start()

                partner_copy(slot, i, d).start()

        def both(k, carry):
            @pl.when(k >= 2)
            def _():
                wait_partner(t + (k % 2) * (NT - 1))

            slot = t + (k % 2) * (NT - 1) + (k // 2) * NZ
            lower = jnp.where(k % 2 == 0, z - t, z + t - NZ) >= 0
            attend(slot, lower)
            return carry

        lax.fori_loop(0, 4, both, 0)
        return carry

    lax.fori_loop(1, NT, ring_step, 0)

    for i, d in enumerate(DORDER):
        arrived(i < 2, NT, last, i, d)
        partner_copy(last, i, d).start()
    lower = z >= NT
    attend(last, lower)
    wait_partner(last)
    attend(NZ + last, lower)

    for xq in range(NX):
        ctx[xq] = (o_s[xq] / l_s[xq]).astype(BF16)
    wrap = jnp.where(zc == 0, 1, 0)
    before = (zc + NZC - 1) % NZC
    for d in (1, 3, 2):
        cp = remote(
            ctx.at[x_abs(d)], win.at[x, pl.ds(0, CD), :], o_send.at[d - 1], o_recv.at[NX - d - 1], at_seq(x_peer(d)))
        cp.start()
        sends.append(cp)
    for d in DORDER:
        target = x_abs(d) * NZC + before
        cp = remote(
            ctx.at[(x + d + wrap) % NX], win.at[x, pl.ds(CD, CD), :], n_send.at[d], n_recv.at[(NX - d) % NX], at_seq(target))
        cp.start()
        sends.append(cp)
    win[x, pl.ds(0, CD), :] = ctx[x]
    for d in (1, 3, 2):
        dst = win.at[x_abs(d), pl.ds(0, CD), :]
        remote(dst, dst, o_send.at[0], o_recv.at[d - 1], at_seq(partner)).wait_recv()
    for d in DORDER:
        dst = win.at[x_abs(d), pl.ds(CD, CD), :]
        remote(dst, dst, n_send.at[0], n_recv.at[d], at_seq(partner)).wait_recv()

    lane = lax.broadcasted_iota(jnp.int32, (1, seqs), 1)
    lens = lengths[...]
    start = jnp.sum(jnp.where(lane < s, lens, 0), axis=1, keepdims=True) - s * CD
    count = jnp.sum(jnp.where(lane == s, lens, 0), axis=1, keepdims=True)
    row = lax.broadcasted_iota(jnp.int32, (2 * CD, 2 * CD), 0)
    col = lax.broadcasted_iota(jnp.int32, (2 * CD, 2 * CD), 1)
    pick = jnp.where((col == row + start) & (row < count), 1.0, 0.0).astype(BF16)
    for h in range(NX):
        out[:, pl.ds(h * HD, HD)] = jnp.dot(pick, win[h], preferred_element_type=F32).astype(BF16)

    bnd.wait_send()
    for cp in ss + sends:
        cp.wait_send()
    for i, d in enumerate(DORDER):
        def sent(t, carry):
            for up in (True, False):
                ring_copy(up, 0, t, 0, i, d).wait_send()
            return carry

        lax.fori_loop(1, NT, sent, 0)
        ring_copy(i < 2, 0, NT, 0, i, d).wait_send()

        def passed(slot, carry):
            partner_copy(slot, i, d).wait_send()
            return carry

        lax.fori_loop(0, NZ, passed, 0)


def shards(seqs, tokens, w_short, w_query, w_key, w_value, owner_lengths):
    rows, part_width = tokens.shape
    CD = rows // 3
    width = part_width * NY
    features = w_query.shape[1]
    NZ = seqs // (2 * NX)
    NT = NZ // 2
    half = part_width // 2
    dma = pltpu.SemaphoreType.DMA
    vmem = pl.BlockSpec(memory_space=pltpu.VMEM)
    hbm = pl.BlockSpec(memory_space=pl.ANY)
    return pl.pallas_call(
        functools.partial(layer_kernel, seqs, width),
        out_shape=jax.ShapeDtypeStruct((2 * CD, features), BF16),
        in_specs=[hbm, vmem, hbm, hbm, hbm, vmem],
        out_specs=vmem,
        scratch_shapes=[
            pltpu.VMEM((rows, part_width), BF16),
            pltpu.VMEM((part_width // 128, rows + 8, 128), F32),
            pltpu.VMEM((part_width // 128, CD, 128), F32),
            pltpu.VMEM((128, 128), F32),
            pltpu.VMEM((4, 8, 128), F32),
            pltpu.VMEM((4, 2, CD, half), BF16),
            pltpu.VMEM((4, 3, part_width, features), BF16),
            pltpu.VMEM((3, CD, features), F32),
            pltpu.VMEM((NX, 2, CD, HD), BF16),
            pltpu.VMEM((NX, CD, HD), BF16),
            pltpu.VMEM((2 * NZ, 2, NX * CD, HD), BF16),
            pltpu.VMEM((NX, CD, HD), BF16),
            pltpu.VMEM((NX, CD, HD), F32),
            pltpu.VMEM((NX, CD, HD), F32),
            pltpu.VMEM((NX, CD, HD), F32),
            pltpu.VMEM((NX, CD, HD), BF16),
            pltpu.VMEM((NX, 2 * CD, HD), BF16),
            dma((2,)), dma((4, 3)), dma((2,)), dma((3,)), dma((3,)), dma((6,)), dma((6,)),
            dma((3,)), dma((3,)), dma((3,)), dma((3,)),
            dma((NT, 4)), dma((NT, 4)), dma((NT, 4)), dma((NT, 4)),
            dma((NZ, 4)), dma((NZ, 4)), dma((3,)), dma((3,)), dma((4,)), dma((4,)),
        ],
        compiler_params=pltpu.CompilerParams(
            collective_id=0, has_side_effects=True, vmem_limit_bytes=56 * 1024 * 1024),
        name="layer",
    )(tokens, w_short, w_query, w_key, w_value, owner_lengths.reshape(1, seqs))


def solution(mesh):
    return jax.shard_map(
        functools.partial(shards, mesh.shape["seq"]),
        mesh=mesh,
        in_specs=(
            P("seq", "head"),
            P(None, "head"),
            P(None, "head"),
            P(None, "head"),
            P(None, "head"),
            P(),
        ),
        out_specs=P("seq", "head"),
        check_vma=False,
    )
```

time: 277 us -> 67.4 us (0.24)
  the two profiles are of different devices: /device:TPU:199 before, /device:TPU:1 now
where the time goes in v1:
time: 67.4 us; the launch traced here: 67.3 us
  Pallas kernels  65.6 us (97%)
  local copies, waits for them, and re-layouts  1.64 us (2%)
    pallas_call x1, Pallas kernels, shards(): pl.pallas_call(functools.partial(layer_kernel, seqs, width), out_shape=ja...  65.6 us
    unnamed x1, local copies, waits for them, and re-layouts  1.64 us

profile of v1, /device:TPU:1, one launch (start us, length us, event | category | flops | bytes accessed | tf_op | source)
XLA Modules:
  0.0 67.3 jit_solution(17453144513684719096)
XLA Ops:
  0.0 65.6 %layer.1 = bf16[224,512]{1,0:T(8,128)(2,1)} custom-call(bf16[336,1024]{1,0:T(8,128)(2,1)} %tokens.1, f32[3,1024]{1,0:T(4,128)} %w_short.1, bf16[4096,512]{1,0:T(8,128)(2,1)} %w_q.1, bf16[4096,512]{1,0:T(8,128)(2,1)} %w_k.1, bf16[4096,512]{1,0:T(8,128)(2,1)} %w_v.1, s32[1,64]{1,0:T(1,128)} %bitcast.1), custom_call_target="tpu_custom_call" | custom-call | tf_op jit(solution)/shard_map/layer/pallas_call | solution.py:390
  65.6 1.6 %copy.8 = bf16[224,512]{1,0:T(8,128)(2,1)} copy(bf16[224,512]{1,0:T(8,128)(2,1)} %layer.1) | data formatting | bytes 458752

commit v2 on v1

--- a/solution.py
+++ b/solution.py
@@ -22,7 +22,7 @@
     tokens, w_short, w_q, w_k, w_v, lengths,
     out,
     tok, tok32, pooled, part, sums, coarse, weights, acc, kv_out, q_out, kv, q_all,
-    m_s, l_s, o_s, ctx, win,
+    q_t, m_s, l_s, o_s, ctx, win,
     tok_sem, w_sem, bnd_sem, ss_send, ss_recv, y_send, y_recv,
     s2_send, s2_recv, q_send, q_recv, cw_send, cw_recv, ccw_send, ccw_recv,
     pt_send, pt_recv, o_send, o_recv, n_send, n_recv,
@@ -238,38 +238,48 @@
     for d in (1, 3, 2):
         remote(q_all.at[x_abs(d)], q_all.at[x_abs(d)], q_send.at[0], q_recv.at[d - 1], at_seq(partner)).wait_recv()
 
-    inverse = 1.0 / math.sqrt(HD)
+    slope = math.log2(math.e) / math.sqrt(HD)
+    for xq in range(NX):
+        padded = jnp.concatenate([q_all[xq], jnp.zeros((128 - CD, HD), BF16)], axis=0) if CD < 128 else q_all[xq]
+        q_t[:, pl.ds(xq * 128, 128)] = padded.T
+
+    def allow(sc, pair, xk, allowed, first):
+        if xk < 2 * pair:
+            return sc
+        lane = lax.broadcasted_iota(jnp.int32, (CD, 256), 1)
+        lower = xk == 2 * pair
+        if first:
+            row = lax.broadcasted_iota(jnp.int32, (CD, 256), 0)
+            ok = (lane >= 128) | (row <= lane) if lower else (lane >= 128) & (row <= lane - 128)
+        else:
+            ok = lane >= (jnp.where(allowed, 0, 128) if lower else jnp.where(allowed, 128, 256))
+        return jnp.where(ok, sc, MASKED)
 
     def attend(slot, allowed, first=False):
-        for xq in range(NX):
-            nk = (xq + 1) * CD
-            keys = kv[slot, 0, pl.ds(0, nk), :]
-            values = kv[slot, 1, pl.ds(0, nk), :]
-            sc = lax.dot_general(q_all[xq], keys, (((1,), (1,)), ((), ())), preferred_element_type=F32) * inverse
-            column = lax.broadcasted_iota(jnp.int32, (CD, nk), 1)
+        for pair in range(NX // 2):
+            blocks = 2 * pair + 2
+            keys = pl.ds(0, blocks * CD)
+            lanes = pl.ds(pair * 256, 256)
+            sc = jnp.dot(kv[slot, 0, keys, :], q_t[:, lanes], preferred_element_type=F32)
+            parts = [allow(sc[k * CD:(k + 1) * CD], pair, k, allowed, first) for k in range(blocks)]
+            tops = [jnp.max(p.reshape(CD // 8, 8, 256), axis=0) for p in parts]
+            top = jnp.max(functools.reduce(jnp.maximum, tops), axis=0, keepdims=True)
+            if not first:
+                old = m_s[0:1, lanes]
+                top = jnp.maximum(old, top)
+                alpha = jnp.exp2((old - top) * slope)
+            m_s[:, lanes] = jnp.broadcast_to(top, (8, 256))
+            w = [jnp.exp2((p - top) * slope) for p in parts]
+            lw = functools.reduce(jnp.add, [jnp.sum(p.reshape(CD // 8, 8, 256), axis=0) for p in w])
+            rounded = jnp.concatenate([p.astype(BF16) for p in w], axis=0)
+            added = lax.dot_general(
+                kv[slot, 1, keys, :], rounded, (((0,), (0,)), ((), ())), preferred_element_type=F32)
             if first:
-                limit = lax.broadcasted_iota(jnp.int32, (CD, nk), 0) + (xq * CD + 1)
+                l_s[:, lanes] = lw
+                o_s[:, lanes] = added
             else:
-                limit = jnp.where(allowed, nk, xq * CD)
-            sc = jnp.where(column < limit, sc, MASKED)
-            top = jnp.max(sc, axis=1, keepdims=True)
-            if not first:
-                old = m_s[xq]
-                new = jnp.maximum(old, top)
-                alpha = jnp.exp(old - new)
-                m_s[xq] = new
-                top = new[:, 0:1]
-            else:
-                m_s[xq] = jnp.broadcast_to(top, (CD, HD))
-            w = jnp.exp(sc - top)
-            added = jnp.dot(w.astype(BF16), values, preferred_element_type=F32)
-            lw = jnp.sum(w, axis=1, keepdims=True)
-            if first:
-                l_s[xq] = jnp.broadcast_to(lw, (CD, HD))
-                o_s[xq] = added
-            else:
-                l_s[xq] = l_s[xq] * alpha + lw
-                o_s[xq] = o_s[xq] * alpha + added
+                l_s[:, lanes] = l_s[:, lanes] * alpha + lw
+                o_s[:, lanes] = o_s[:, lanes] * alpha + added
 
     def wait_partner(slot):
         for i, d in enumerate(DORDER):
@@ -325,7 +335,9 @@
     attend(NZ + last, lower)
 
     for xq in range(NX):
-        ctx[xq] = (o_s[xq] / l_s[xq]).astype(BF16)
+        lanes = pl.ds(xq * 128, 128)
+        totals = jnp.sum(l_s[:, lanes], axis=0, keepdims=True)
+        ctx[xq] = (o_s[:, lanes] / totals).T[0:CD].astype(BF16)
     wrap = jnp.where(zc == 0, 1, 0)
     before = (zc + NZC - 1) % NZC
     for d in (1, 3, 2):
@@ -405,9 +417,10 @@
             pltpu.VMEM((NX, CD, HD), BF16),
             pltpu.VMEM((2 * NZ, 2, NX * CD, HD), BF16),
             pltpu.VMEM((NX, CD, HD), BF16),
-            pltpu.VMEM((NX, CD, HD), F32),
-            pltpu.VMEM((NX, CD, HD), F32),
-            pltpu.VMEM((NX, CD, HD), F32),
+            pltpu.VMEM((HD, NX * 128), BF16),
+            pltpu.VMEM((8, NX * 128), F32),
+            pltpu.VMEM((8, NX * 128), F32),
+            pltpu.VMEM((HD, NX * 128), F32),
             pltpu.VMEM((NX, CD, HD), BF16),
             pltpu.VMEM((NX, 2 * CD, HD), BF16),
             dma((2,)), dma((4, 3)), dma((2,)), dma((3,)), dma((3,)), dma((6,)), dma((6,)),

time: 67.4 us -> 60.9 us (0.904)
  Pallas kernels: 65.6 us -> 59.1 us
    pallas_call x1, Pallas kernels: 65.6 us -> 59.1 us  [shards(): pl.pallas_call(functools.partial(layer_kernel, seqs, width), out_shape=ja...]
where the time goes in v2:
time: 60.9 us; the launch traced here: 60.8 us
  Pallas kernels  59.1 us (97%)
  local copies, waits for them, and re-layouts  1.64 us (3%)
    pallas_call x1, Pallas kernels, shards(): pl.pallas_call(functools.partial(layer_kernel, seqs, width), out_shape=ja...  59.1 us
    unnamed x1, local copies, waits for them, and re-layouts  1.64 us

profile of v2, /device:TPU:1, one launch (start us, length us, event | category | flops | bytes accessed | tf_op | source)
XLA Modules:
  0.0 60.8 jit_solution(10719822579926622751)
XLA Ops:
  0.0 59.1 %layer.1 = bf16[224,512]{1,0:T(8,128)(2,1)} custom-call(bf16[336,1024]{1,0:T(8,128)(2,1)} %tokens.1, f32[3,1024]{1,0:T(4,128)} %w_short.1, bf16[4096,512]{1,0:T(8,128)(2,1)} %w_q.1, bf16[4096,512]{1,0:T(8,128)(2,1)} %w_k.1, bf16[4096,512]{1,0:T(8,128)(2,1)} %w_v.1, s32[1,64]{1,0:T(1,128)} %bitcast.1), custom_call_target="tpu_custom_call" | custom-call | tf_op jit(solution)/shard_map/layer/pallas_call | solution.py:402
  59.1 1.6 %copy.8 = bf16[224,512]{1,0:T(8,128)(2,1)} copy(bf16[224,512]{1,0:T(8,128)(2,1)} %layer.1) | data formatting | bytes 458752

commit v3 on v2

--- a/solution.py
+++ b/solution.py
@@ -19,9 +19,9 @@
 
 def layer_kernel(
     seqs, width,
-    tokens, w_short, w_q, w_k, w_v, lengths,
+    tokens, w_short_hbm, w_q, w_k, w_v, lengths_hbm,
     out,
-    tok, tok32, pooled, part, sums, coarse, weights, acc, kv_out, q_out, kv, q_all,
+    w_short, lengths, tok, tok32, pooled, part, sums, coarse, weights, acc, kv_out, q_out, kv, q_all,
     q_t, m_s, l_s, o_s, ctx, win,
     tok_sem, w_sem, bnd_sem, ss_send, ss_recv, y_send, y_recv,
     s2_send, s2_recv, q_send, q_recv, cw_send, cw_recv, ccw_send, ccw_recv,
@@ -76,8 +76,10 @@
         tokens.at[pl.ds(rows - tail, tail)], tok.at[pl.ds(rows - tail, tail)], tok_sem.at[0])
     head_copy = pltpu.make_async_copy(
         tokens.at[pl.ds(0, rows - tail)], tok.at[pl.ds(0, rows - tail)], tok_sem.at[1])
-    tail_copy.start()
-    head_copy.start()
+    short_copy = pltpu.make_async_copy(w_short_hbm, w_short, tok_sem.at[2])
+    lengths_copy = pltpu.make_async_copy(lengths_hbm, lengths, tok_sem.at[3])
+    for cp in (tail_copy, head_copy, short_copy, lengths_copy):
+        cp.start()
     y_of_slot = [y, (y + 3) % NY, (y + 1) % NY, (y + 2) % NY]
     w_copies = []
     for slot in range(4):
@@ -104,6 +106,7 @@
     def _():
         tok32[:, pl.ds(0, 8), :] = jnp.zeros((lane_blocks, 8, 128), F32)
 
+    short_copy.wait()
     part[...] = jnp.zeros_like(part)
     square = jnp.zeros((CD, 128), F32)
     for b in range(lane_blocks):
@@ -360,6 +363,7 @@
         remote(dst, dst, n_send.at[0], n_recv.at[d], at_seq(partner)).wait_recv()
 
     lane = lax.broadcasted_iota(jnp.int32, (1, seqs), 1)
+    lengths_copy.wait()
     lens = lengths[...]
     start = jnp.sum(jnp.where(lane < s, lens, 0), axis=1, keepdims=True) - s * CD
     count = jnp.sum(jnp.where(lane == s, lens, 0), axis=1, keepdims=True)
@@ -401,10 +405,12 @@
     hbm = pl.BlockSpec(memory_space=pl.ANY)
     return pl.pallas_call(
         functools.partial(layer_kernel, seqs, width),
-        out_shape=jax.ShapeDtypeStruct((2 * CD, features), BF16),
-        in_specs=[hbm, vmem, hbm, hbm, hbm, vmem],
+        out_shape=pltpu.VMEM((2 * CD, features), BF16),
+        in_specs=[hbm, hbm, hbm, hbm, hbm, hbm],
         out_specs=vmem,
         scratch_shapes=[
+            pltpu.VMEM((3, part_width), F32),
+            pltpu.VMEM((1, seqs), jnp.int32),
             pltpu.VMEM((rows, part_width), BF16),
             pltpu.VMEM((part_width // 128, rows + 8, 128), F32),
             pltpu.VMEM((part_width // 128, CD, 128), F32),
@@ -423,7 +429,7 @@
             pltpu.VMEM((HD, NX * 128), F32),
             pltpu.VMEM((NX, CD, HD), BF16),
             pltpu.VMEM((NX, 2 * CD, HD), BF16),
-            dma((2,)), dma((4, 3)), dma((2,)), dma((3,)), dma((3,)), dma((6,)), dma((6,)),
+            dma((4,)), dma((4, 3)), dma((2,)), dma((3,)), dma((3,)), dma((6,)), dma((6,)),
             dma((3,)), dma((3,)), dma((3,)), dma((3,)),
             dma((NT, 4)), dma((NT, 4)), dma((NT, 4)), dma((NT, 4)),
             dma((NZ, 4)), dma((NZ, 4)), dma((3,)), dma((3,)), dma((4,)), dma((4,)),

time: 60.9 us -> 58.1 us (0.954)
  Pallas kernels: 59.1 us -> 57.4 us
  local copies, waits for them, and re-layouts: 1.64 us -> 0.69 us
    pallas_call x1, Pallas kernels: 59.1 us -> 57.4 us  [shards(): pl.pallas_call(functools.partial(layer_kernel, seqs, width), out_shape=pl...]
    unnamed x1, local copies, waits for them, and re-layouts: 1.64 us -> 0.69 us
where the time goes in v3:
time: 58.1 us
  Pallas kernels  57.4 us (99%)
  local copies, waits for them, and re-layouts  0.69 us (1%)
    pallas_call x1, Pallas kernels, shards(): pl.pallas_call(functools.partial(layer_kernel, seqs, width), out_shape=pl...  57.4 us

profile of v3, /device:TPU:1, one launch (start us, length us, event | category | flops | bytes accessed | tf_op | source)
XLA Modules:
  0.0 58.1 jit_solution(10233226980736413731)
XLA Ops:
  0.0 57.4 %layer.1 = bf16[224,512]{1,0:T(8,128)(2,1)S(1)} custom-call(bf16[336,1024]{1,0:T(8,128)(2,1)} %tokens.1, f32[3,1024]{1,0:T(4,128)} %w_short_hbm.1, bf16[4096,512]{1,0:T(8,128)(2,1)} %w_q.1, bf16[4096,512]{1,0:T(8,128)(2,1)} %w_k.1, bf16[4096,512]{1,0:T(8,128)(2,1)} %w_v.1, s32[1,64]{1,0:T(1,128)} %bitcast.1), custom_call_target="tpu_custom_call" | custom-call | tf_op jit(solution)/shard_map/layer/pallas_call | solution.py:406
  57.4 0.7 %copy.8 = bf16[224,512]{1,0:T(8,128)(2,1)} copy(bf16[224,512]{1,0:T(8,128)(2,1)S(1)} %layer.1) | data formatting | bytes 458752
